TPU v7x, 512 devices: a whole 4x4x16 slice. The times are simulated.
512 devices in a mesh: gx: 32 (over z, core), vert: 16 (over y, x).
Axes of the slice: x: 4, y: 4, z: 16, core: 2. Of those that a mesh axis runs over, the one named last changes fastest.
Arguments:
- distribution: float32 [4096, 32, 256], P('vert', 'gx'), may hold values from -6 to 6
- relax_rate: float32 [32, 256], P('gx'), may hold values from 0.3 to 3
- node_weight: float32 [4096], P('vert'), may hold values from 0.05 to 1
- kernel_tiles: bfloat16 [32, 128, 1536], P('vert'), may hold values from -0.15625 to 0.15625
- tile_cols: int32 [32, 12], P('vert'), may hold values from 0 to 31, as said below
Outputs:
- new_distribution: float32 [4096, 32, 256], P('vert', 'gx')
Inputs may be any that keep to these rules, and one draw needn't show every extreme that they name: `tile_cols`: row block r lists its own block r first; the 12 column blocks listed for one row block are distinct.
All inputs are finite; a program needn't handle non-finite values.
Results may differ from a plain program's by a relative error of at most 0.0021.
Values may be sent and summed in bfloat16 or wider, within the bound.
No kernel may reach another device: no remote copies, remote signals or barrier semaphores. Data moves between devices by JAX's collectives and lax.ppermute only.
A program may use at most 64 MiB of HBM per device.

v0:
```python
import jax
import jax.numpy as jnp
from jax import lax
from jax.sharding import PartitionSpec as P

Q = 16
TILE = 128
NZ = 4
STEPS = 2
V = 4096
RBLK = 32
COURANT_SCALE = 0.3
KERNEL_STEP = 0.5
PRECISE = lax.Precision.HIGHEST


def extended(block, sides, width):
    for axis, dim in sides:
        count = lax.axis_size(axis)
        forward = [(i, i + 1) for i in range(count - 1)]
        forward.append((count - 1, 0))
        backward = [(target, source) for source, target in forward]
        low = lax.ppermute(
            lax.slice_in_dim(block, block.shape[dim] - width, None, axis=dim), axis, forward
        )
        high = lax.ppermute(lax.slice_in_dim(block, 0, width, axis=dim), axis, backward)
        block = jnp.concatenate([low, block, high], axis=dim)
    return block


def node_components(first_node, node_count):
    node_index = first_node + jnp.arange(node_count, dtype=jnp.int32)
    middle = (Q - 1) / 2.0
    speed_x = ((node_index % Q).astype(jnp.float32) - middle) / middle
    speed_y = ((node_index // Q % Q).astype(jnp.float32) - middle) / middle
    speed_z = ((node_index // (Q * Q)).astype(jnp.float32) - middle) / middle
    courant = COURANT_SCALE * jnp.stack([speed_x, speed_y, speed_z])
    squares = speed_x * speed_x + speed_y * speed_y + speed_z * speed_z
    invariants = jnp.stack([jnp.ones_like(speed_x), speed_x, speed_y, speed_z, squares])
    return (courant, invariants)


def gram_inverse(weighted, invariants):
    gram_matrix = jnp.dot(weighted, invariants.T, precision=PRECISE)
    factor = jnp.linalg.cholesky(gram_matrix)
    return jax.scipy.linalg.cho_solve((factor, True), jnp.eye(5, dtype=gram_matrix.dtype))


def advect(source, lower_x, upper_x, courant):
    plane_size = source.shape[-1]
    z_index = jnp.arange(plane_size, dtype=jnp.int32) % NZ
    lower_y = jnp.roll(source, NZ, axis=-1)
    upper_y = jnp.roll(source, -NZ, axis=-1)
    lower_z = jnp.where(
        z_index == 0, jnp.roll(source, 1 - NZ, axis=-1), jnp.roll(source, 1, axis=-1)
    )
    upper_z = jnp.where(
        z_index == NZ - 1, jnp.roll(source, NZ - 1, axis=-1), jnp.roll(source, -1, axis=-1)
    )
    total_flux = jnp.zeros_like(source)
    for component, below, above in (
        (0, lower_x, upper_x),
        (1, lower_y, upper_y),
        (2, lower_z, upper_z),
    ):
        node_speed = courant[component][:, None, None]
        total_flux = (
            total_flux
            + jnp.maximum(node_speed, 0.0) * (source - below)
            + jnp.minimum(node_speed, 0.0) * (above - source)
        )
    return source - total_flux


def apply_kernel(blocks, tile_rows, column_lists):
    cell_count = blocks.shape[-1]

    def one_block(tile_pair):
        tile_row, column_list = tile_pair
        picked = jnp.take(blocks, column_list, axis=0).reshape(-1, cell_count)
        return jnp.dot(tile_row, picked, preferred_element_type=jnp.float32)

    return lax.map(one_block, (tile_rows, column_lists))


def per_device(distribution, relax_rate, node_weight, kernel_tiles, tile_cols):
    node_local, slab_depth, plane_cells = distribution.shape
    cell_count = slab_depth * plane_cells
    first_node = lax.axis_index("vert") * node_local
    courant, invariants = node_components(first_node, node_local)
    all_weights = lax.all_gather(node_weight, "vert", axis=0, tiled=True)
    all_speeds, all_invariants = node_components(0, V)
    all_weighted = all_invariants * all_weights[None, :]
    inverse = gram_inverse(all_weighted, all_invariants)
    relax_share = relax_rate / (1.0 + relax_rate)
    current = distribution
    for step_index in range(STEPS):
        rounded = current.astype(jnp.bfloat16)
        padded = extended(current, (("gx", 1),), 1)
        lower_x = padded[:, :-2]
        upper_x = padded[:, 2:]
        advected = advect(current, lower_x, upper_x, courant)
        gathered = lax.all_gather(
            rounded.reshape(node_local, cell_count), "vert", axis=0, tiled=True
        )
        kernel_term = apply_kernel(
            gathered.reshape(RBLK, TILE, cell_count), kernel_tiles, tile_cols
        )
        explicit = advected + KERNEL_STEP * kernel_term.reshape(current.shape)
        local_weighted = invariants * node_weight[None, :]
        partial_moments = jnp.dot(
            local_weighted, explicit.reshape(node_local, cell_count), precision=PRECISE
        )
        moments = lax.psum(partial_moments, "vert")
        coeffs = jnp.dot(inverse, moments, precision=PRECISE)
        equilibrium = jnp.dot(invariants.T, coeffs, precision=PRECISE).reshape(current.shape)
        current = explicit - relax_share[None] * (explicit - equilibrium)
    return current


def solution(mesh):
    placed = (
        P("vert", "gx", None),
        P("gx", None),
        P("vert"),
        P("vert", None, None),
        P("vert", None),
    )
    return jax.shard_map(
        per_device, mesh=mesh, in_specs=placed, out_specs=P("vert", "gx", None), check_vma=False
    )
```

profile of v0, /device:TPU:32, one launch (start us, length us, event | category | flops | bytes accessed | tf_op | source)
XLA Modules:
  0.0 240.1 jit_solution(10722678696788781217)
XLA Ops:
  6.5 1.1 copy.54
  7.6 0.5 collective-permute-start
  8.1 1.6 copy.68
  9.9 0.1 fusion.55
  10.1 0.1 stack.8
  10.2 23.6 %all-gather.2 = f32[16,1,256]{2,1,0:T(1,128)S(1)} all-gather(f32[1,1,256]{2,1,0:T(1,128)} %bitcast.109), channel_id=1, replica_groups=mesh['gx'=32,'vert'=16] {'vert'}, dimensions={0}, use_global_device_ids=true | all-gather | bytes 17408 | tf_op jit(solution)/shard_map/all_gather | solution.py:91
  33.8 0.4 fusion.44
  34.1 0.1 copy.57
  34.2 0.5 cholesky.17
  34.8 0.6 compare_reduce_fusion
  35.4 0.6 fusion.59
  36.1 0.4 custom-call.10
  36.6 0.7 add_divide_fusion
  37.3 0.2 fusion.60
  37.5 0.1 fusion.62
  37.7 0.7 fusion.82
  38.5 36.6 %all-gather.6.cloned.1.call-done = bf16[4096,1,256]{2,0,1:T(8,128)(2,1)} async-done(((bf16[256,1,256]{2,0,1:T(8,128)(2,1)}), bf16[4096,1,256]{2,0,1:T(8,128)(2,1)}) %all-gather.6.cloned.1.call-update) | async-done | bytes 2097168 | tf_op jit(solution)/shard_map/all_gather | solution.py:103
  75.1 5.3 %while.20 = (s32[]{:T(128)}, f32[2,128,256]{2,1,0:T(8,128)S(1)}, bf16[2,128,1536]{2,1,0:T(8,128)(2,1)S(1)}, s32[2,12]{1,0:T(2,128)S(1)}, bf16[32,128,256]{2,1,0:T(8,128)(2,1)}, /*index=5*/s32[]{:T(128)}) while((s32[]{:T(128)}, f32[2,128,256]{2,1,0:T(8,128)S(1)}, bf16[2,128,1536]{2,1,0:T(8,128)(2,1)S(1)}, s32[2,12]{1,0:T(2,128)S(1)}, ...), condition=%wide.region_1.3_spmd, body=%wide.region_0.2_spmd.sunk | while | flops 101057608 | bytes 4461865 | solution.py:83
  75.1 2.2 gather_fusion
  77.3 0.1 broadcast_select_fusion.4
  77.5 0.3 fusion.111
  77.8 2.2 gather_fusion
  80.0 0.1 broadcast_select_fusion.4
  80.2 0.3 fusion.111
  80.5 0.1 copy.64
  80.6 1.4 fusion.22
  82.0 0.3 fusion.42
  82.3 38.7 %psum.14 = f32[5,256]{1,0:T(8,128)S(1)} all-reduce(f32[5,256]{1,0:T(8,128)S(1)} %fusion.42), channel_id=1, replica_groups=mesh['gx'=32,'vert'=16] {'vert'}, use_global_device_ids=true, to_apply=%region_4.6 | all-reduce | flops 1280 | bytes 10240 | tf_op jit(solution)/shard_map/psum | solution.py:114
  121.0 0.1 fusion.89
  121.1 1.1 fusion.88
  122.3 0.5 collective-permute-start.2
  122.9 0.7 fusion.79
  123.6 58.2 %all-gather.8.cloned.1.call-done = bf16[4096,1,256]{0,2,1:T(8,128)(2,1)} async-done(((bf16[256,1,256]{0,2,1:T(8,128)(2,1)}), bf16[4096,1,256]{0,2,1:T(8,128)(2,1)}) %all-gather.8.cloned.1.call-update) | async-done | bytes 2097168 | tf_op jit(solution)/shard_map/all_gather | solution.py:103
  181.8 4.1 %copy.65 = bf16[4096,1,256]{2,0,1:T(8,128)(2,1)} copy(bf16[4096,1,256]{0,2,1:T(8,128)(2,1)} %all-gather.8.cloned.1.call-done) | data formatting | bytes 4194304 | tf_op jit(solution)/shard_map/while | solution.py:83
  185.9 5.3 %while.21 = (s32[]{:T(128)}, f32[2,128,256]{2,1,0:T(8,128)S(1)}, bf16[2,128,1536]{2,1,0:T(8,128)(2,1)S(1)}, s32[2,12]{1,0:T(2,128)S(1)}, bf16[32,128,256]{2,1,0:T(8,128)(2,1)}, /*index=5*/s32[]{:T(128)}) while((s32[]{:T(128)}, f32[2,128,256]{2,1,0:T(8,128)S(1)}, bf16[2,128,1536]{2,1,0:T(8,128)(2,1)S(1)}, s32[2,12]{1,0:T(2,128)S(1)}, ...), condition=%wide.region_6.8_spmd, body=%wide.region_5.7_spmd.sunk | while | flops 101057608 | bytes 4461865 | solution.py:83
  186.0 2.2 gather_fusion.1
  188.2 0.1 broadcast_select_fusion.5
  188.3 0.3 fusion.114
  188.6 2.2 gather_fusion.1
  190.8 0.1 broadcast_select_fusion.5
  191.0 0.3 fusion.114
  191.3 0.1 copy.66
  191.4 1.4 fusion.34
  192.8 0.3 fusion.40
  193.1 38.7 %psum.15 = f32[5,256]{1,0:T(8,128)S(1)} all-reduce(f32[5,256]{1,0:T(8,128)S(1)} %fusion.40), channel_id=1, replica_groups=mesh['gx'=32,'vert'=16] {'vert'}, use_global_device_ids=true, to_apply=%region_7.9 | all-reduce | flops 1280 | bytes 10240 | tf_op jit(solution)/shard_map/psum | solution.py:114
  231.8 0.1 fusion.90
  231.9 0.4 fusion.15
  232.4 0.8 copy.62
  (49 shorter events, 0.7 us)
Async XLA Ops:
  6.5 68.5 %all-gather.6.cloned.1.call-start = ((), (), s32[]{:S(2)}) async-start(), calls=%async_computation | async-start | bytes 2228224 | tf_op jit(solution)/shard_map/all_gather | solution.py:103
  7.6 73.0 %collective-permute-start.1 = (f32[256,1,256]{0,2,1:T(8,128)S(1)}, f32[256,1,256]{0,2,1:T(8,128)}, u32[]{:S(2)}, u32[]{:S(2)}) collective-permute-start(f32[256,1,256]{0,2,1:T(8,128)S(1)} %copy.54), channel_id=1, source_target_pairs={{16,0},{32,16},{48,32},{64,48},{80,64},{96,80},{112,96},{128,112},... | collective-permute-start | bytes 786440 | tf_op jit(solution)/shard_map/ppermute | solution.py:26
  7.6 73.0 %collective-permute-start = (f32[256,1,256]{0,2,1:T(8,128)S(1)}, f32[256,1,256]{0,2,1:T(8,128)}, u32[]{:S(2)}, u32[]{:S(2)}) collective-permute-start(f32[256,1,256]{0,2,1:T(8,128)S(1)} %copy.54), channel_id=1, source_target_pairs={{0,16},{16,32},{32,48},{48,64},{64,80},{80,96},{96,112},{112,128},... | collective-permute-start | bytes 786440 | tf_op jit(solution)/shard_map/ppermute | solution.py:23
  9.8 65.3 %copy-start = (bf16[2,128,1536]{2,1,0:T(8,128)(2,1)S(1)}, bf16[2,128,1536]{2,1,0:T(8,128)(2,1)}, u32[]{:S(2)}) copy-start(bf16[2,128,1536]{2,1,0:T(8,128)(2,1)} %param.14) | copy-start | bytes 2359300
  9.8 65.3 %copy-start.1 = (s32[2,12]{1,0:T(2,128)S(1)}, s32[2,12]{1,0:T(2,128)}, u32[]{:S(2)}) copy-start(s32[2,12]{1,0:T(2,128)} %param.15) | copy-start | bytes 292
  9.8 172.0 %all-gather.8.cloned.1.call-start = ((), (), s32[]{:S(2)}) async-start(), calls=%async_computation.1 | async-start | bytes 2228224 | tf_op jit(solution)/shard_map/all_gather | solution.py:103
  80.4 1.6 copy-start.2
  122.2 69.2 %collective-permute-start.3 = (f32[256,1,256]{0,2,1:T(8,128)S(1)}, f32[256,1,256]{0,2,1:T(8,128)}, u32[]{:S(2)}, u32[]{:S(2)}) collective-permute-start(f32[256,1,256]{0,2,1:T(8,128)S(1)} %get-tuple-element.127), channel_id=1, source_target_pairs={{16,0},{32,16},{48,32},{64,48},{80,64},{96,80},{112,96},{128,112},... | collective-permute-start | bytes 786440 | tf_op jit(solution)/shard_map/ppermute | solution.py:26
  122.3 69.2 %collective-permute-start.2 = (f32[256,1,256]{0,2,1:T(8,128)S(1)}, f32[256,1,256]{0,2,1:T(8,128)}, u32[]{:S(2)}, u32[]{:S(2)}) collective-permute-start(f32[256,1,256]{0,2,1:T(8,128)S(1)} %get-tuple-element.127), channel_id=1, source_target_pairs={{0,16},{16,32},{32,48},{48,64},{64,80},{80,96},{96,112},{112,128},... | collective-permute-start | bytes 786440 | tf_op jit(solution)/shard_map/ppermute | solution.py:23
Sparse Core Ops, SparseCore 0:
  10.4 64.6 all-gather.5
  122.3 59.4 all-gather.7
where the time goes:
time: 241 us; the launch traced here: 240 us
  blocking collectives  101 us (42%)
  waiting for transfers between devices  94.9 us (39%)
  local copies, waits for them, and re-layouts  18.6 us (8%)
  between operations  13.7 us (6%)
  other arithmetic  6.55 us (3%)
  matrix products  4.07 us (2%)
    all_gather x2, waiting for transfers between devices, per_device(): lax.all_gather(rounded.reshape(node_local, cell_count), 'vert', axis=0, t...  94.8 us
    psum x2, blocking collectives, per_device(): moments = lax.psum(partial_moments, 'vert')  77.4 us
    all_gather x1, blocking collectives, per_device(): all_weights = lax.all_gather(node_weight, 'vert', axis=0, tiled=True)  23.6 us
    gather x4, local copies, waits for them, and re-layouts, one_block(): picked = jnp.take(blocks, column_list, axis=0).reshape(-1, cell_count)  8.75 us
  transfers between devices with their start and end apart: 6, of which 2 were waited for; matrix products, arithmetic and copies ran while one was open for 9% of the time, Pallas kernels for 0%

commit v1 on v0

--- a/solution.py
+++ b/solution.py
@@ -88,7 +88,9 @@
     cell_count = slab_depth * plane_cells
     first_node = lax.axis_index("vert") * node_local
     courant, invariants = node_components(first_node, node_local)
-    all_weights = lax.all_gather(node_weight, "vert", axis=0, tiled=True)
+    all_weights = jnp.concatenate(
+        lax.all_to_all(jnp.stack([node_weight] * lax.axis_size("vert")), "vert", 0, 0), axis=0
+    )
     all_speeds, all_invariants = node_components(0, V)
     all_weighted = all_invariants * all_weights[None, :]
     inverse = gram_inverse(all_weighted, all_invariants)

time: 241 us -> 251 us (1.041)
  waiting for transfers between devices: 94.9 us -> 120 us
  blocking collectives: 101 us -> 77.4 us
  starting transfers between devices: 1.07 us -> 8.15 us
    all_gather x1 -> x0, blocking collectives: 23.6 us -> none  [per_device(): all_weights = lax.all_gather(node_weight, 'vert', axis=0, tiled=True)]
    all_gather x2, waiting for transfers between devices: 94.8 us -> 116 us  [per_device(): lax.all_gather(rounded.reshape(node_local, cell_count), 'vert', axis=0, t...]
    all_to_all x0 -> x1, starting transfers between devices: none -> 7.03 us  [per_device(): lax.all_to_all(jnp.stack([node_weight] * lax.axis_size('vert')), 'vert',...]
    all_to_all x0 -> x1, waiting for transfers between devices: none -> 3.75 us  [per_device(): lax.all_to_all(jnp.stack([node_weight] * lax.axis_size('vert')), 'vert',...]
  transfers between devices with their start and end apart: 6 -> 7, of which waited for: 2 -> 3; matrix products, arithmetic and copies ran while one was open for 9% -> 9% of each run, Pallas kernels for 0% -> 0%
where the time goes in v1:
time: 251 us; the launch traced here: 250 us
  waiting for transfers between devices  120 us (48%)
  blocking collectives  77.4 us (31%)
  local copies, waits for them, and re-layouts  19.9 us (8%)
  between operations  13.7 us (5%)
  starting transfers between devices  8.15 us (3%)
  other arithmetic  6.53 us (3%)
  matrix products  4.09 us (2%)
    all_gather x2, waiting for transfers between devices, per_device(): lax.all_gather(rounded.reshape(node_local, cell_count), 'vert', axis=0, t...  116 us
    psum x2, blocking collectives, per_device(): moments = lax.psum(partial_moments, 'vert')  77.4 us
    gather x4, local copies, waits for them, and re-layouts, one_block(): picked = jnp.take(blocks, column_list, axis=0).reshape(-1, cell_count)  8.75 us
    all_to_all x1, starting transfers between devices, per_device(): lax.all_to_all(jnp.stack([node_weight] * lax.axis_size('vert')), 'vert',...  7.03 us
  transfers between devices with their start and end apart: 7, of which 3 were waited for; matrix products, arithmetic and copies ran while one was open for 9% of the time, Pallas kernels for 0%

profile of v1, /device:TPU:32, one launch (start us, length us, event | category | flops | bytes accessed | tf_op | source)
XLA Modules:
  0.0 250.0 jit_solution(10390912753168074338)
XLA Ops:
  6.5 1.1 copy.54
  7.6 0.5 collective-permute-start
  8.1 1.3 stack.11
  9.4 7.0 %all-to-all-start = ((f32[16,1,256]{2,1,0:T(1,128)}), f32[16,1,256]{2,1,0:T(1,128)S(1)}, u32[]{:S(2)}, u32[]{:S(2)}) async-start(f32[16,1,256]{2,1,0:T(1,128)} %stack.11), calls=%async_computation | async-start | bytes 32768 | tf_op jit(solution)/shard_map/all_to_all | solution.py:92
  16.5 1.6 copy.68
  18.3 0.7 add_divide_fusion
  19.2 0.7 fusion.82
  20.2 0.1 stack.10
  20.3 3.8 %all-to-all-done = f32[16,1,256]{2,1,0:T(1,128)S(1)} async-done(((f32[16,1,256]{2,1,0:T(1,128)}), f32[16,1,256]{2,1,0:T(1,128)S(1)}, u32[]{:S(2)}, u32[]{:S(2)}) %all-to-all-start) | async-done | bytes 16416 | tf_op jit(solution)/shard_map/all_to_all | solution.py:92
  24.1 0.3 fusion.44
  24.5 0.5 cholesky.17
  25.0 0.7 compare_reduce_fusion
  25.7 0.6 fusion.59
  26.3 0.4 custom-call.10
  26.7 0.2 fusion.60
  26.8 0.1 fusion.62
  27.0 58.1 %all-gather.5.cloned.1.call-done = bf16[4096,1,256]{2,0,1:T(8,128)(2,1)} async-done(((bf16[256,1,256]{2,0,1:T(8,128)(2,1)}), bf16[4096,1,256]{2,0,1:T(8,128)(2,1)}) %all-gather.5.cloned.1.call-update) | async-done | bytes 2097168 | tf_op jit(solution)/shard_map/all_gather | solution.py:105
  85.1 5.3 %while.20 = (s32[]{:T(128)}, f32[2,128,256]{2,1,0:T(8,128)S(1)}, bf16[2,128,1536]{2,1,0:T(8,128)(2,1)S(1)}, s32[2,12]{1,0:T(2,128)S(1)}, bf16[32,128,256]{2,1,0:T(8,128)(2,1)}, /*index=5*/s32[]{:T(128)}) while((s32[]{:T(128)}, f32[2,128,256]{2,1,0:T(8,128)S(1)}, bf16[2,128,1536]{2,1,0:T(8,128)(2,1)S(1)}, s32[2,12]{1,0:T(2,128)S(1)}, ...), condition=%wide.region_1.3_spmd, body=%wide.region_0.2_spmd.sunk | while | flops 101057608 | bytes 4461865 | solution.py:83
  85.1 2.2 gather_fusion
  87.3 0.1 broadcast_select_fusion.4
  87.5 0.3 fusion.111
  87.8 2.2 gather_fusion
  90.0 0.1 broadcast_select_fusion.4
  90.1 0.3 fusion.111
  90.5 0.1 copy.64
  90.6 1.4 fusion.22
  92.0 0.3 fusion.42
  92.3 38.7 %psum.14 = f32[5,256]{1,0:T(8,128)S(1)} all-reduce(f32[5,256]{1,0:T(8,128)S(1)} %fusion.42), channel_id=1, replica_groups=mesh['gx'=32,'vert'=16] {'vert'}, use_global_device_ids=true, to_apply=%region_4.6 | all-reduce | flops 1280 | bytes 10240 | tf_op jit(solution)/shard_map/psum | solution.py:116
  131.0 0.1 fusion.89
  131.1 1.1 fusion.88
  132.2 0.5 collective-permute-start.2
  132.9 0.7 fusion.79
  133.6 58.2 %all-gather.7.cloned.1.call-done = bf16[4096,1,256]{0,2,1:T(8,128)(2,1)} async-done(((bf16[256,1,256]{0,2,1:T(8,128)(2,1)}), bf16[4096,1,256]{0,2,1:T(8,128)(2,1)}) %all-gather.7.cloned.1.call-update) | async-done | bytes 2097168 | tf_op jit(solution)/shard_map/all_gather | solution.py:105
  191.8 4.1 %copy.65 = bf16[4096,1,256]{2,0,1:T(8,128)(2,1)} copy(bf16[4096,1,256]{0,2,1:T(8,128)(2,1)} %all-gather.7.cloned.1.call-done) | data formatting | bytes 4194304 | tf_op jit(solution)/shard_map/while | solution.py:83
  195.9 5.3 %while.21 = (s32[]{:T(128)}, f32[2,128,256]{2,1,0:T(8,128)S(1)}, bf16[2,128,1536]{2,1,0:T(8,128)(2,1)S(1)}, s32[2,12]{1,0:T(2,128)S(1)}, bf16[32,128,256]{2,1,0:T(8,128)(2,1)}, /*index=5*/s32[]{:T(128)}) while((s32[]{:T(128)}, f32[2,128,256]{2,1,0:T(8,128)S(1)}, bf16[2,128,1536]{2,1,0:T(8,128)(2,1)S(1)}, s32[2,12]{1,0:T(2,128)S(1)}, ...), condition=%wide.region_6.8_spmd, body=%wide.region_5.7_spmd.sunk | while | flops 101057608 | bytes 4461865 | solution.py:83
  195.9 2.2 gather_fusion.1
  198.1 0.1 broadcast_select_fusion.5
  198.3 0.3 fusion.114
  198.6 2.2 gather_fusion.1
  200.8 0.1 broadcast_select_fusion.5
  201.0 0.3 fusion.114
  201.3 0.1 copy.66
  201.4 1.4 fusion.34
  202.8 0.3 fusion.40
  203.1 38.7 %psum.15 = f32[5,256]{1,0:T(8,128)S(1)} all-reduce(f32[5,256]{1,0:T(8,128)S(1)} %fusion.40), channel_id=1, replica_groups=mesh['gx'=32,'vert'=16] {'vert'}, use_global_device_ids=true, to_apply=%region_7.9 | all-reduce | flops 1280 | bytes 10240 | tf_op jit(solution)/shard_map/psum | solution.py:116
  241.8 0.1 fusion.90
  241.9 0.4 fusion.15
  242.4 0.8 copy.62
  (51 shorter events, 0.9 us)
Async XLA Ops:
  7.6 83.0 %collective-permute-start.1 = (f32[256,1,256]{0,2,1:T(8,128)S(1)}, f32[256,1,256]{0,2,1:T(8,128)}, u32[]{:S(2)}, u32[]{:S(2)}) collective-permute-start(f32[256,1,256]{0,2,1:T(8,128)S(1)} %copy.54), channel_id=1, source_target_pairs={{16,0},{32,16},{48,32},{64,48},{80,64},{96,80},{112,96},{128,112},... | collective-permute-start | bytes 786440 | tf_op jit(solution)/shard_map/ppermute | solution.py:26
  7.6 83.0 %collective-permute-start = (f32[256,1,256]{0,2,1:T(8,128)S(1)}, f32[256,1,256]{0,2,1:T(8,128)}, u32[]{:S(2)}, u32[]{:S(2)}) collective-permute-start(f32[256,1,256]{0,2,1:T(8,128)S(1)} %copy.54), channel_id=1, source_target_pairs={{0,16},{16,32},{32,48},{48,64},{64,80},{80,96},{96,112},{112,128},... | collective-permute-start | bytes 786440 | tf_op jit(solution)/shard_map/ppermute | solution.py:23
  9.4 14.6 %all-to-all-start = ((f32[16,1,256]{2,1,0:T(1,128)}), f32[16,1,256]{2,1,0:T(1,128)S(1)}, u32[]{:S(2)}, u32[]{:S(2)}) async-start(f32[16,1,256]{2,1,0:T(1,128)} %stack.11), calls=%async_computation | async-start | bytes 32768 | tf_op jit(solution)/shard_map/all_to_all | solution.py:92
  16.5 68.6 %all-gather.5.cloned.1.call-start = ((), (), s32[]{:S(2)}) async-start(), calls=%async_computation.1 | async-start | bytes 2228224 | tf_op jit(solution)/shard_map/all_gather | solution.py:105
  18.2 66.9 %copy-start = (bf16[2,128,1536]{2,1,0:T(8,128)(2,1)S(1)}, bf16[2,128,1536]{2,1,0:T(8,128)(2,1)}, u32[]{:S(2)}) copy-start(bf16[2,128,1536]{2,1,0:T(8,128)(2,1)} %param.14) | copy-start | bytes 2359300
  18.2 66.9 %copy-start.1 = (s32[2,12]{1,0:T(2,128)S(1)}, s32[2,12]{1,0:T(2,128)}, u32[]{:S(2)}) copy-start(s32[2,12]{1,0:T(2,128)} %param.15) | copy-start | bytes 292
  18.2 173.6 %all-gather.7.cloned.1.call-start = ((), (), s32[]{:S(2)}) async-start(), calls=%async_computation.2 | async-start | bytes 2228224 | tf_op jit(solution)/shard_map/all_gather | solution.py:105
  90.4 1.6 copy-start.2
  132.2 69.2 %collective-permute-start.3 = (f32[256,1,256]{0,2,1:T(8,128)S(1)}, f32[256,1,256]{0,2,1:T(8,128)}, u32[]{:S(2)}, u32[]{:S(2)}) collective-permute-start(f32[256,1,256]{0,2,1:T(8,128)S(1)} %get-tuple-element.127), channel_id=1, source_target_pairs={{16,0},{32,16},{48,32},{64,48},{80,64},{96,80},{112,96},{128,112},... | collective-permute-start | bytes 786440 | tf_op jit(solution)/shard_map/ppermute | solution.py:26
  132.2 69.2 %collective-permute-start.2 = (f32[256,1,256]{0,2,1:T(8,128)S(1)}, f32[256,1,256]{0,2,1:T(8,128)}, u32[]{:S(2)}, u32[]{:S(2)}) collective-permute-start(f32[256,1,256]{0,2,1:T(8,128)S(1)} %get-tuple-element.127), channel_id=1, source_target_pairs={{0,16},{16,32},{32,48},{48,64},{64,80},{80,96},{96,112},{112,128},... | collective-permute-start | bytes 786440 | tf_op jit(solution)/shard_map/ppermute | solution.py:23
Sparse Core Ops, SparseCore 0:
  20.3 64.6 all-gather.4
  132.3 59.4 all-gather.6
